TPU v7x, 32 devices: a whole 2x2x4 slice. The times are simulated.
32 devices in a mesh: group: 2 (over y), tm: 4 (over z), seq: 2 (over x), mp: 2 (over core).
Axes of the slice: x: 2, y: 2, z: 4, core: 2. Of those that a mesh axis runs over, the one named last changes fastest.
Arguments:
- states: bfloat16 [8, 128, 5120], P(('group', 'tm'), 'seq'), parts along dimension 0, may hold values from -6 to 6
- start_step: int32 [2], P('group'), parts along dimension 0, may hold values from 0 to 96
- w_qkv: bfloat16 [3, 5120, 3072], P(None, 'tm', ('seq', 'mp')), may hold values from -0.078125 to 0.078125
- qk_gain: float32 [2, 3072], P(None, ('seq', 'mp')), may hold values from 0.25 to 1.75
- w_out: bfloat16 [5120, 3072], P('tm', ('seq', 'mp')), may hold values from -0.109375 to 0.109375
- time_proj: bfloat16 [256, 15360], P('tm'), may hold values from -0.375 to 0.375
Outputs:
- displacement: float32 [8, 128, 5120], P(('group', 'tm'), 'seq', 'mp'), parts along dimension 0
There are 2 independent parts, one for each index of `group`. A program takes and returns all parts, laid end to end along the dimension named above; an argument that names none is the same for every part. Nothing has to cross between parts.
Inputs may be any that keep to these rules, and one draw needn't show every extreme that they name: `start_step`: the window lies inside the trajectory.
All inputs are finite; a program needn't handle non-finite values.
Results may differ from a plain program's by a relative error of at most 0.0029.
Values may be sent and summed in bfloat16 or wider, within the bound.
No kernel may reach another device: no remote copies, remote signals or barrier semaphores. Data moves between devices by JAX's collectives and lax.ppermute only.
A program may use at most 128 MiB of HBM per device.

v0:
```python
import jax
import jax.numpy as jnp
from jax import lax
from jax.sharding import PartitionSpec as P

HEAD_DIM = 128
FREQ = 256
STEPS = 100
sample_shift = 5.0
norm_eps = 1e-06


def from_behind(block, axis, distance):
    devices = range(lax.axis_size(axis))
    route = [(i - distance, i) for i in devices if i - distance in devices]
    return lax.ppermute(block, axis, route)


def sigma_of(index):
    unit = 1.0 - index.astype(jnp.float32) / jnp.float32(STEPS)
    return sample_shift * unit / (1.0 + (sample_shift - 1.0) * unit)


def embed_time(sigma_now):
    half_freq = FREQ // 2
    ranks = jnp.arange(half_freq).astype(jnp.float32)
    freqs = jnp.exp(-jnp.log(jnp.float32(10000.0)) * ranks / jnp.float32(half_freq))
    angles = (1000.0 * sigma_now)[:, None] * freqs[None, :]
    return jnp.concatenate([jnp.cos(angles), jnp.sin(angles)], axis=1).astype(jnp.bfloat16)


def head_norm(values, gain, frames, seq_len, heads_dev):
    shaped = values.reshape(frames, seq_len, heads_dev, HEAD_DIM)
    meansq = jnp.mean(shaped * shaped, axis=-1, keepdims=True)
    scaled = shaped * lax.rsqrt(meansq + norm_eps) * gain.reshape(heads_dev, HEAD_DIM)
    return scaled.astype(jnp.bfloat16)


def attend(query, keys, values):
    frames, seq_len, heads_dev, head_size = query.shape
    block = min(seq_len, 512)
    blocks = seq_len // block
    inv_root = 1.0 / jnp.sqrt(jnp.float32(head_size))
    stacked = query.reshape(frames, blocks, block, heads_dev, head_size).transpose(1, 0, 2, 3, 4)

    def one_block(q_block):
        scores = (
            jnp.einsum("wqhd,wkhd->whqk", q_block, keys, preferred_element_type=jnp.float32)
            * inv_root
        )
        expo = jnp.exp(scores)
        probs = (expo / jnp.sum(expo, axis=-1, keepdims=True)).astype(jnp.bfloat16)
        return jnp.einsum(
            "whqk,wkhd->wqhd", probs, values, preferred_element_type=jnp.float32
        ).astype(jnp.bfloat16)

    result = lax.map(one_block, stacked)
    return result.transpose(1, 0, 2, 3, 4).reshape(frames, seq_len, heads_dev * head_size)


def on_device(states, start_step, w_qkv, qk_gain, w_out, time_proj):
    frames, tok, width = states.shape
    n_tm = lax.axis_size("tm")
    n_mp = lax.axis_size("mp")
    window = frames * n_tm
    tm_pos = lax.axis_index("tm")
    steps_idx = start_step[0] + jnp.arange(window)
    sigma_now = sigma_of(steps_idx)
    step_size = sigma_of(steps_idx + 1) - sigma_now
    emb = embed_time(sigma_now)
    freq_rows = time_proj.shape[0]
    emb_cols = lax.dynamic_slice_in_dim(emb, tm_pos * freq_rows, freq_rows, 1)
    modulation = lax.psum_scatter(
        jnp.dot(emb_cols, time_proj, preferred_element_type=jnp.float32),
        "tm",
        scatter_dimension=0,
        tiled=True,
    )
    shift = modulation[:, :width]
    scale = modulation[:, width : 2 * width]
    gate = modulation[:, 2 * width :]
    field = states.astype(jnp.float32)
    mean = jnp.mean(field, axis=-1, keepdims=True)
    centred = field - mean
    var = jnp.mean(centred * centred, axis=-1, keepdims=True)
    normed = centred * lax.rsqrt(var + norm_eps)
    hidden = (normed * (1.0 + scale[:, None, :]) + shift[:, None, :]).astype(jnp.bfloat16)
    whole = lax.all_gather(hidden, "seq", axis=1, tiled=True)
    seq_len = whole.shape[1]
    flat = whole.reshape(frames * seq_len, width)
    head_cols = w_qkv.shape[2]
    heads_dev = head_cols // HEAD_DIM
    proj = jnp.einsum(
        "rd,cdh->crh",
        flat,
        lax.all_gather(w_qkv, "tm", axis=1, tiled=True),
        preferred_element_type=jnp.float32,
    )
    query = head_norm(proj[0], qk_gain[0], frames, seq_len, heads_dev)
    keys = head_norm(proj[1], qk_gain[1], frames, seq_len, heads_dev)
    values = proj[2].astype(jnp.bfloat16).reshape(frames, seq_len, heads_dev, HEAD_DIM)
    attn = attend(query, keys, values)
    out_full = lax.all_gather(w_out, "tm", axis=0, tiled=True)
    half_width = width // n_mp
    rows = frames * tok
    first = jnp.int32(0) // rows
    pieces = []
    for offset in range(rows * lax.axis_size(("seq", "mp")) // rows):
        owner = first + offset
        segment = owner // n_mp
        column = owner % n_mp
        tokens_part = lax.dynamic_slice_in_dim(attn, segment * tok, tok, 1)
        weight_part = lax.dynamic_slice_in_dim(out_full, column * half_width, half_width, 0)
        product = jnp.einsum(
            "tsh,eh->tse", tokens_part, weight_part, preferred_element_type=jnp.float32
        )
        pieces.append(product.reshape(rows, half_width))
    out_part = lax.psum_scatter(
        jnp.concatenate(pieces, axis=0), ("seq", "mp"), scatter_dimension=0, tiled=True
    ).reshape(frames, tok, half_width)
    gate_own = lax.dynamic_slice_in_dim(gate, lax.axis_index("mp") * half_width, half_width, 1)
    own_steps = lax.dynamic_slice_in_dim(step_size, tm_pos * frames, frames, 0)
    drift = gate_own[:, None, :] * out_part
    increments = own_steps[:, None, None] * drift
    local_sums = jnp.cumsum(increments, axis=0)
    block_total = local_sums[-1]
    running = block_total
    for level in range((n_tm - 1).bit_length()):
        running = running + from_behind(running, "tm", 1 << level)
    before = running - block_total
    return before[None, :, :] + local_sums


def solution(mesh):
    return jax.shard_map(
        on_device,
        mesh=mesh,
        in_specs=(
            P(("group", "tm"), "seq", None),
            P("group"),
            P(None, "tm", ("seq", "mp")),
            P(None, ("seq", "mp")),
            P("tm", ("seq", "mp")),
            P("tm", None),
        ),
        out_specs=P(("group", "tm"), "seq", "mp"),
        check_vma=False,
    )
```

profile of v0, /device:TPU:25, one launch (start us, length us, event | category | flops | bytes accessed | tf_op | source)
XLA Modules:
  0.0 721.7 jit_solution(13477119722304982495)
XLA Ops:
  7.4 0.5 divide_subtract_fusion
  8.3 1.1 fusion.26
  10.1 0.6 dynamic-slice.1
  10.7 32.4 %all-reduce.3.cloned.1.call-done = f32[4,15360]{1,0:T(4,128)} async-done(((f32[4,15360]{1,0:T(4,128)}), f32[4,15360]{1,0:T(4,128)}) %all-reduce.3.cloned.1.call-update) | async-done | bytes 245776
  43.0 1.7 dynamic-slice_add_fusion
  44.7 1.1 fusion.13
  45.9 0.7 all-gather.6.cloned.1.call-update
  46.7 0.5 all-gather.8.cloned.1.call-update
  47.3 25.9 %all-gather.4.cloned.1.call-done = bf16[1,128,5120]{2,1,0:T(8,128)(2,1)} async-done(((bf16[1,64,5120]{2,1,0:T(8,128)(2,1)}), bf16[1,128,5120]{2,1,0:T(8,128)(2,1)}) %all-gather.4.cloned.1.call-update) | async-done | bytes 1310736 | tf_op jit(solution)/shard_map/all_gather | solution.py:88
  73.2 398.3 %all-gather.6.cloned.1.call-done = bf16[3,5120,768]{2,1,0:T(8,128)(2,1)} async-done(((bf16[3,1280,768]{2,1,0:T(8,128)(2,1)}), bf16[3,5120,768]{2,1,0:T(8,128)(2,1)}) %all-gather.6.cloned.1.call-update) | async-done | bytes 23592976 | tf_op jit(solution)/shard_map/all_gather | solution.py:96
  471.4 10.0 %convolution_bitcast_fusion = f32[3,128,768]{2,1,0:T(8,128)S(1)} fusion(bf16[3,5120,768]{2,1,0:T(8,128)(2,1)} %all-gather.6.cloned.1.call-done, bf16[1,128,5120]{2,1,0:T(8,128)(2,1)} %all-gather.4.cloned.1.call-done), kind=kOutput, calls=%fused_computation.13 | convolution fusion | flops 3019898880 | bytes 26083328 | tf_op jit(solution)/shard_map/rd,cdh->crh/dot_general | solution.py:93
  481.4 0.7 slice.45
  482.3 0.9 copy.23
  483.3 1.1 reduce_sum.49
  484.8 1.1 copy.19
  486.7 125.4 %all-gather.8.cloned.1.call-done = bf16[5120,768]{1,0:T(8,128)(2,1)} async-done(((bf16[1280,768]{1,0:T(8,128)(2,1)}), bf16[5120,768]{1,0:T(8,128)(2,1)}) %all-gather.8.cloned.1.call-update) | async-done | bytes 7864336 | tf_op jit(solution)/shard_map/all_gather | solution.py:103
  612.1 3.6 fusion.2
  615.7 3.6 fusion.4
  619.3 1.3 fusion.6
  620.6 1.5 fusion
  622.1 1.7 pad_maximum_fusion
  623.8 0.6 copy-done.5
  624.3 0.6 dynamic_slice.28
  624.9 1.5 dynamic-slice_reduce_fusion
  626.4 32.9 %reduce-scatter.2.cloned.1.call-done = f32[64,2560]{1,0:T(8,128)} async-done(((f32[256,2560]{1,0:T(8,128)}), f32[64,2560]{1,0:T(8,128)}) %reduce-scatter.2.cloned.1.call-update) | async-done | bytes 655376 | tf_op jit(solution)/shard_map/reduce_scatter | solution.py:118
  659.4 1.8 multiply_multiply_fusion
  661.1 1.3 collective-permute-start
  662.4 16.1 %collective-permute-done = f32[64,2560]{1,0:T(8,128)S(1)} collective-permute-done((f32[64,2560]{1,0:T(8,128)S(1)}, f32[64,2560]{1,0:T(8,128)S(1)}, u32[]{:S(2)}, u32[]{:S(2)}) %collective-permute-start) | collective-permute-done | bytes 655392 | tf_op jit(solution)/shard_map/ppermute | solution.py:16
  678.5 1.7 fusion.35
  680.2 1.3 collective-permute-start.1
  681.5 32.1 %collective-permute-done.1 = f32[64,2560]{1,0:T(8,128)S(1)} collective-permute-done((f32[64,2560]{1,0:T(8,128)S(1)}, f32[64,2560]{1,0:T(8,128)S(1)}, u32[]{:S(2)}, u32[]{:S(2)}) %collective-permute-start.1) | collective-permute-done | bytes 655392 | tf_op jit(solution)/shard_map/ppermute | solution.py:16
  713.7 1.5 fusion.16
  (37 shorter events, 2.6 us)
Async XLA Ops:
  6.5 1.8 copy-start
  6.5 3.5 copy-start.6
  6.5 3.0 copy-start.2
  6.5 36.5 %all-reduce.3.cloned.1.call-start = ((), (), s32[]{:S(2)}) async-start(), calls=%async_computation.5 | async-start | bytes 491520
  9.5 63.7 %all-gather.4.cloned.1.call-start = ((), (), s32[]{:S(2)}) async-start(), calls=%async_computation.1 | async-start | bytes 1966080 | tf_op jit(solution)/shard_map/all_gather | solution.py:88
  45.9 1.4 copy-start.4
  45.9 425.6 %all-gather.6.cloned.1.call-start = ((), (), s32[]{:S(2)}) async-start(), calls=%async_computation.2 | async-start | bytes 29491200 | tf_op jit(solution)/shard_map/all_gather | solution.py:96
  46.6 565.5 %all-gather.8.cloned.1.call-start = ((), (), s32[]{:S(2)}) async-start(), calls=%async_computation.3 | async-start | bytes 9830400 | tf_op jit(solution)/shard_map/all_gather | solution.py:103
  47.2 612.2 %reduce-scatter.2.cloned.1.call-start = ((), (), s32[]{:S(2)}) async-start(), calls=%async_computation.4 | async-start | bytes 3276800 | tf_op jit(solution)/shard_map/reduce_scatter | solution.py:118
  612.1 7.1 copy-start.1
  623.8 0.6 copy-start.5
  659.4 54.3 %copy-start.3 = (f32[64,2560]{1,0:T(8,128)S(1)}, f32[64,2560]{1,0:T(8,128)}, u32[]{:S(2)}) copy-start(f32[64,2560]{1,0:T(8,128)} %reduce-scatter.2.cloned.1.call-done) | copy-start | bytes 1966084
  661.1 17.4 %collective-permute-start = (f32[64,2560]{1,0:T(8,128)S(1)}, f32[64,2560]{1,0:T(8,128)S(1)}, u32[]{:S(2)}, u32[]{:S(2)}) collective-permute-start(f32[64,2560]{1,0:T(8,128)S(1)} %multiply_multiply_fusion), channel_id=1, source_target_pairs={{0,4},{4,8},{8,12},{1,5},{5,9},{9,13},{2,6},{6,10},{10,14},{3,7},{... | collective-permute-start | bytes 1966088 | tf_op jit(solution)/shard_map/ppermute | solution.py:16
  680.2 33.4 %collective-permute-start.1 = (f32[64,2560]{1,0:T(8,128)S(1)}, f32[64,2560]{1,0:T(8,128)S(1)}, u32[]{:S(2)}, u32[]{:S(2)}) collective-permute-start(f32[64,2560]{1,0:T(8,128)S(1)} %fusion.35), channel_id=1, source_target_pairs={{0,8},{4,12},{1,9},{5,13},{2,10},{6,14},{3,11},{7,15},{16,24},{20,... | collective-permute-start | bytes 1966088 | tf_op jit(solution)/shard_map/ppermute | solution.py:16
Sparse Core Ops, SparseCore 0:
  9.7 33.3 all-reduce.2
  46.0 27.1 all-gather.3
  74.7 396.6 all-gather.5
  472.9 139.2 all-gather.7
  623.9 35.4 reduce-scatter.1
where the time goes:
time: 722 us
  waiting for transfers between devices  664 us (92%)
  matrix products  21.8 us (3%)
  between operations  14.1 us (2%)
  other arithmetic  12 us (2%)
    all_gather x1, waiting for transfers between devices, on_device(): lax.all_gather(w_qkv, 'tm', axis=1, tiled=True)  398 us
    all_gather x1, waiting for transfers between devices, on_device(): out_full = lax.all_gather(w_out, 'tm', axis=0, tiled=True)  125 us
    ppermute x2, waiting for transfers between devices, from_behind(): return lax.ppermute(block, axis, route)  48.2 us
    unnamed x6, waiting for transfers between devices  33.6 us
    reduce_scatter x1, waiting for transfers between devices, on_device(): lax.psum_scatter(jnp.concatenate(pieces, axis=0), ('seq', 'mp'), scatter_...  32.9 us
    all_gather x1, waiting for transfers between devices, on_device(): whole = lax.all_gather(hidden, 'seq', axis=1, tiled=True)  25.9 us
  transfers between devices with their start and end apart: 7, of which 7 were waited for; matrix products, arithmetic and copies ran while one was open for 3% of the time, Pallas kernels for 0%

commit v1 on v0

--- a/solution.py
+++ b/solution.py
@@ -8,6 +8,26 @@
 STEPS = 100
 sample_shift = 5.0
 norm_eps = 1e-06
+
+
+def _store_runs(xin, link_axis, raw):
+    passed, val, current_block = (
+        jax.lax.axis_size(link_axis),
+        jax.lax.axis_index(link_axis),
+        xin.shape[1],
+    )
+    buffers = [(k0, (k0 + 1) % passed) for k0 in range(passed)]
+    cards = [(k0, (k0 - 1) % passed) for k0 in range(passed)]
+    placed = passed // 2
+    extra = response = xin
+    right_arr = raw(xin, val * current_block)
+    for j0 in range(1, placed + 1):
+        extra = jax.lax.ppermute(extra, link_axis, buffers)
+        if j0 < passed - placed:
+            response = jax.lax.ppermute(response, link_axis, cards)
+            right_arr = right_arr + raw(response, (val + j0) % passed * current_block)
+        right_arr = right_arr + raw(extra, (val - j0) % passed * current_block)
+    return right_arr
 
 
 def from_behind(block, axis, distance):
@@ -90,11 +110,15 @@
     flat = whole.reshape(frames * seq_len, width)
     head_cols = w_qkv.shape[2]
     heads_dev = head_cols // HEAD_DIM
-    proj = jnp.einsum(
-        "rd,cdh->crh",
-        flat,
-        lax.all_gather(w_qkv, "tm", axis=1, tiled=True),
-        preferred_element_type=jnp.float32,
+    proj = _store_runs(
+        w_qkv,
+        "tm",
+        lambda shard, offset_2: jnp.einsum(
+            "rd,cdh->crh",
+            lax.dynamic_slice_in_dim(flat, offset_2, shard.shape[1], axis=1),
+            shard,
+            preferred_element_type=jnp.float32,
+        ),
     )
     query = head_norm(proj[0], qk_gain[0], frames, seq_len, heads_dev)
     keys = head_norm(proj[1], qk_gain[1], frames, seq_len, heads_dev)

time: 722 us -> 665 us (0.921)
  waiting for transfers between devices: 664 us -> 599 us
    all_gather x1 -> x0, waiting for transfers between devices: 398 us -> none  [on_device(): lax.all_gather(w_qkv, 'tm', axis=1, tiled=True)]
    ppermute x0 -> x3, waiting for transfers between devices: none -> 345 us  [the longest x1 186 us: _store_runs(): response = jax.lax.ppermute(response, link_axis, cards)]
    all_gather x1, waiting for transfers between devices: 125 us -> 0.02 us  [on_device(): out_full = lax.all_gather(w_out, 'tm', axis=0, tiled=True)]
    unnamed x6 -> x5, waiting for transfers between devices: 33.6 us -> 150 us
    dot_general x1 -> x4, matrix products: 9.97 us -> 15 us  [on_device(): jnp.einsum('rd,cdh->crh', lax.dynamic_slice_in_dim(flat, offset_2, shard....]
  transfers between devices with their start and end apart: 7 -> 9, of which waited for: 7 -> 7; matrix products, arithmetic and copies ran while one was open for 3% -> 4% of each run, Pallas kernels for 0% -> 0%
where the time goes in v1:
time: 665 us
  waiting for transfers between devices  599 us (90%)
  matrix products  26.8 us (4%)
  between operations  14.2 us (2%)
  other arithmetic  12 us (2%)
  local copies, waits for them, and re-layouts  6.9 us (1%)
    ppermute x1, waiting for transfers between devices, _store_runs(): response = jax.lax.ppermute(response, link_axis, cards)  186 us
    ppermute x2, waiting for transfers between devices, _store_runs(): extra = jax.lax.ppermute(extra, link_axis, buffers)  158 us
    unnamed x5, waiting for transfers between devices  150 us
    ppermute x2, waiting for transfers between devices, from_behind(): return lax.ppermute(block, axis, route)  48.2 us
    reduce_scatter x1, waiting for transfers between devices, on_device(): lax.psum_scatter(jnp.concatenate(pieces, axis=0), ('seq', 'mp'), scatter_...  33.1 us
    all_gather x1, waiting for transfers between devices, on_device(): whole = lax.all_gather(hidden, 'seq', axis=1, tiled=True)  23.2 us
    dot_general x4, matrix products, on_device(): jnp.einsum('rd,cdh->crh', lax.dynamic_slice_in_dim(flat, offset_2, shard....  15 us
  transfers between devices with their start and end apart: 9, of which 7 were waited for; matrix products, arithmetic and copies ran while one was open for 4% of the time, Pallas kernels for 0%

profile of v1, /device:TPU:25, one launch (start us, length us, event | category | flops | bytes accessed | tf_op | source)
XLA Modules:
  0.0 664.8 jit_solution(16927126989954970895)
XLA Ops:
  8.3 1.1 fusion.39
  10.8 148.8 %all-reduce.3.cloned.1.call-done = f32[4,15360]{1,0:T(4,128)} async-done(((f32[4,15360]{1,0:T(4,128)}), f32[4,15360]{1,0:T(4,128)}) %all-reduce.3.cloned.1.call-update) | async-done | bytes 245776
  159.6 1.7 dynamic-slice_add_fusion
  161.4 1.1 fusion.14
  162.6 0.7 all-gather.5.cloned.1.call-update
  163.3 1.2 collective-permute-start
  164.5 2.1 collective-permute-start.2
  166.7 23.2 %all-gather.3.cloned.1.call-done = bf16[1,128,5120]{2,1,0:T(8,128)(2,1)} async-done(((bf16[1,64,5120]{2,1,0:T(8,128)(2,1)}), bf16[1,128,5120]{2,1,0:T(8,128)(2,1)}) %all-gather.3.cloned.1.call-update) | async-done | bytes 1310736 | tf_op jit(solution)/shard_map/all_gather | solution.py:108
  189.8 3.8 fusion.20
  193.7 186.4 %collective-permute-done = bf16[3,1280,768]{2,1,0:T(8,128)(2,1)} collective-permute-done((bf16[3,1280,768]{2,1,0:T(8,128)(2,1)}, bf16[3,1280,768]{2,1,0:T(8,128)(2,1)}, u32[]{:S(2)}, u32[]{:S(2)}) %collective-permute-start) | collective-permute-done | bytes 5898272 | tf_op jit(solution)/shard_map/ppermute | solution.py:27
  380.0 3.8 convolution_add_fusion.2
  383.8 3.7 convolution_add_fusion.1
  387.5 158.5 %collective-permute-done.2 = bf16[3,1280,768]{2,1,0:T(8,128)(2,1)} collective-permute-done((bf16[3,1280,768]{2,1,0:T(8,128)(2,1)}, bf16[3,1280,768]{2,1,0:T(8,128)(2,1)}, u32[]{:S(2)}, u32[]{:S(2)}) %collective-permute-start.2) | collective-permute-done | bytes 5898272 | tf_op jit(solution)/shard_map/ppermute | solution.py:25
  546.0 3.7 fusion.10
  549.7 0.7 slice.45
  550.5 0.9 copy.23
  551.6 1.0 reduce_sum.49
  553.0 1.1 copy.19
  554.9 3.6 fusion.2
  558.5 3.6 fusion.4
  562.1 1.3 fusion.6
  563.4 1.5 fusion
  564.8 1.7 pad_maximum_fusion
  567.7 1.6 dynamic-slice_reduce_fusion
  569.3 33.1 %reduce-scatter.2.cloned.1.call-done = f32[64,2560]{1,0:T(8,128)} async-done(((f32[256,2560]{1,0:T(8,128)}), f32[64,2560]{1,0:T(8,128)}) %reduce-scatter.2.cloned.1.call-update) | async-done | bytes 655376 | tf_op jit(solution)/shard_map/reduce_scatter | solution.py:142
  602.4 1.8 multiply_multiply_fusion
  604.2 1.3 collective-permute-start.3
  605.5 16.0 %collective-permute-done.3 = f32[64,2560]{1,0:T(8,128)S(1)} collective-permute-done((f32[64,2560]{1,0:T(8,128)S(1)}, f32[64,2560]{1,0:T(8,128)S(1)}, u32[]{:S(2)}, u32[]{:S(2)}) %collective-permute-start.3) | collective-permute-done | bytes 655392 | tf_op jit(solution)/shard_map/ppermute | solution.py:36
  621.5 1.7 fusion.50
  623.3 1.3 collective-permute-start.4
  624.6 32.2 %collective-permute-done.4 = f32[64,2560]{1,0:T(8,128)S(1)} collective-permute-done((f32[64,2560]{1,0:T(8,128)S(1)}, f32[64,2560]{1,0:T(8,128)S(1)}, u32[]{:S(2)}, u32[]{:S(2)}) %collective-permute-start.4) | collective-permute-done | bytes 655392 | tf_op jit(solution)/shard_map/ppermute | solution.py:36
  656.7 1.5 fusion.16
  (45 shorter events, 5.0 us)
Async XLA Ops:
  6.5 1.8 copy-start
  6.5 3.6 copy-start.7
  6.5 3.0 copy-start.2
  6.5 153.1 %all-reduce.3.cloned.1.call-start = ((), (), s32[]{:S(2)}) async-start(), calls=%async_computation.4 | async-start | bytes 491520
  9.5 180.4 %all-gather.3.cloned.1.call-start = ((), (), s32[]{:S(2)}) async-start(), calls=%async_computation.1 | async-start | bytes 1966080 | tf_op jit(solution)/shard_map/all_gather | solution.py:108
  9.5 155.0 %collective-permute-start.1 = (bf16[3,1280,768]{2,1,0:T(8,128)(2,1)}, bf16[3,1280,768]{2,1,0:T(8,128)(2,1)}, u32[]{:S(2)}, u32[]{:S(2)}) collective-permute-start(bf16[3,1280,768]{2,1,0:T(8,128)(2,1)} %param.8), channel_id=1, source_target_pairs={{0,4},{4,8},{8,12},{12,0},{1,5},{5,9},{9,13},{13,1},{2,6},{6,10},{... | collective-permute-start | bytes 17694728 | tf_op jit(solution)/shard_map/ppermute | solution.py:25
  161.3 5.3 copy-start.5
  162.5 392.4 %all-gather.5.cloned.1.call-start = ((), (), s32[]{:S(2)}) async-start(), calls=%async_computation.2 | async-start | bytes 9830400 | tf_op jit(solution)/shard_map/all_gather | solution.py:127
  163.3 439.2 %reduce-scatter.2.cloned.1.call-start = ((), (), s32[]{:S(2)}) async-start(), calls=%async_computation.3 | async-start | bytes 3276800 | tf_op jit(solution)/shard_map/reduce_scatter | solution.py:142
  163.3 216.7 %collective-permute-start = (bf16[3,1280,768]{2,1,0:T(8,128)(2,1)}, bf16[3,1280,768]{2,1,0:T(8,128)(2,1)}, u32[]{:S(2)}, u32[]{:S(2)}) collective-permute-start(bf16[3,1280,768]{2,1,0:T(8,128)(2,1)} %param.8), channel_id=1, source_target_pairs={{0,12},{4,0},{8,4},{12,8},{1,13},{5,1},{9,5},{13,9},{2,14},{6,2},{... | collective-permute-start | bytes 17694728 | tf_op jit(solution)/shard_map/ppermute | solution.py:27
  164.5 381.5 %collective-permute-start.2 = (bf16[3,1280,768]{2,1,0:T(8,128)(2,1)}, bf16[3,1280,768]{2,1,0:T(8,128)(2,1)}, u32[]{:S(2)}, u32[]{:S(2)}) collective-permute-start(bf16[3,1280,768]{2,1,0:T(8,128)(2,1)} %collective-permute-done.1), channel_id=1, source_target_pairs={{0,4},{4,8},{8,12},{12,0},{1,5},{5,9},{9,13},{13,1},{2,6},{6,10},{... | collective-permute-start | bytes 17694728 | tf_op jit(solution)/shard_map/ppermute | solution.py:25
  189.8 190.2 %copy-start.4 = (bf16[1,128,5120]{2,1,0:T(8,128)(2,1)S(1)}, bf16[1,128,5120]{2,1,0:T(8,128)(2,1)}, u32[]{:S(2)}) copy-start(bf16[1,128,5120]{2,1,0:T(8,128)(2,1)} %all-gather.3.cloned.1.call-done) | copy-start | bytes 3932164
  554.9 7.2 %copy-start.1 = (bf16[5120,768]{1,0:T(8,128)(2,1)S(1)}, bf16[5120,768]{1,0:T(8,128)(2,1)}, u32[]{:S(2)}) copy-start(bf16[5120,768]{1,0:T(8,128)(2,1)} %all-gather.5.cloned.1.call-done) | copy-start | bytes 23592964
  566.5 0.6 copy-start.6
  602.4 54.3 %copy-start.3 = (f32[64,2560]{1,0:T(8,128)S(1)}, f32[64,2560]{1,0:T(8,128)}, u32[]{:S(2)}) copy-start(f32[64,2560]{1,0:T(8,128)} %reduce-scatter.2.cloned.1.call-done) | copy-start | bytes 1966084
  604.2 17.3 %collective-permute-start.3 = (f32[64,2560]{1,0:T(8,128)S(1)}, f32[64,2560]{1,0:T(8,128)S(1)}, u32[]{:S(2)}, u32[]{:S(2)}) collective-permute-start(f32[64,2560]{1,0:T(8,128)S(1)} %multiply_multiply_fusion), channel_id=1, source_target_pairs={{0,4},{4,8},{8,12},{1,5},{5,9},{9,13},{2,6},{6,10},{10,14},{3,7},{... | collective-permute-start | bytes 1966088 | tf_op jit(solution)/shard_map/ppermute | solution.py:36
  623.3 33.5 %collective-permute-start.4 = (f32[64,2560]{1,0:T(8,128)S(1)}, f32[64,2560]{1,0:T(8,128)S(1)}, u32[]{:S(2)}, u32[]{:S(2)}) collective-permute-start(f32[64,2560]{1,0:T(8,128)S(1)} %fusion.50), channel_id=1, source_target_pairs={{0,8},{4,12},{1,9},{5,13},{2,10},{6,14},{3,11},{7,15},{16,24},{20,... | collective-permute-start | bytes 1966088 | tf_op jit(solution)/shard_map/ppermute | solution.py:36
Sparse Core Ops, SparseCore 0:
  9.7 149.8 all-reduce.2
  162.6 27.1 all-gather.2
  191.4 293.0 all-gather.4
  566.7 35.6 reduce-scatter.1
